TPU v7x, 32 devices: a whole 2x2x4 slice. The times are simulated.
32 devices in a mesh: ctx: 8 (over y, x, core), tp: 4 (over z).
Axes of the slice: x: 2, y: 2, z: 4, core: 2. Of those that a mesh axis runs over, the one named last changes fastest.
Arguments:
- queries: bfloat16 [1024, 32, 128], P('ctx', 'tp'), may hold values from -8 to 8
- window_keys: bfloat16 [1024, 4, 128], P('ctx', 'tp'), may hold values from -8 to 8
- window_values: bfloat16 [1024, 4, 128], P('ctx', 'tp'), may hold values from -6 to 6
- anchor_keys: bfloat16 [512, 4, 128], P('ctx', 'tp'), may hold values from -8 to 8
- anchor_values: bfloat16 [512, 4, 128], P('ctx', 'tp'), may hold values from -6 to 6
- passing_rows: int32 [8, 32], replicated, may hold values from 0 to 127, as said below
- block_of_device: int32 [8], replicated, may hold values from 0 to 7, each once
- out_weight: bfloat16 [4096, 4096], P(None, 'tp'), may hold values from -0.09375 to 0.09375
Outputs:
- mixed: bfloat16 [4096, 1024], P('tp', 'ctx')
Inputs may be any that keep to these rules, and one draw needn't show every extreme that they name: `passing_rows`: each row holds 32 different positions. `block_of_device`: every block number appears once.
All inputs are finite; a program needn't handle non-finite values.
Results may differ from a plain program's by a relative error of at most 0.013.
Values may be sent and summed in bfloat16 or wider, within the bound.
No kernel may reach another device: no remote copies, remote signals or barrier semaphores. Data moves between devices by JAX's collectives and lax.ppermute only.
A program may use at most 128 MiB of HBM per device.

v0:
```python
import jax
import jax.numpy as jnp
from jax import lax
from jax.sharding import PartitionSpec as P


def lookup(lookup_table, slot_ids):
    matches = slot_ids[:, None] == jnp.arange(lookup_table.shape[0], dtype=jnp.int32)[None, :]
    return jnp.sum(jnp.where(matches, lookup_table[None, :], 0), axis=1)


def attend(fold_state, grouped, key_rows, value_rows, visible):
    running_max, running_sum, weighted = fold_state
    key_count = key_rows.shape[0]
    score_scale = grouped.shape[-1] ** (-0.5)
    for first_key in range(0, key_count, 1024):
        last_key = min(first_key + 1024, key_count)
        visible_part = visible[:, first_key:last_key][:, None, None, :]
        scores = (
            jnp.einsum(
                "tgjd,ngd->tgjn",
                grouped,
                key_rows[first_key:last_key],
                preferred_element_type=jnp.float32,
            )
            * score_scale
        )
        scores = jnp.where(visible_part, scores, -1e30)
        new_max = jnp.maximum(running_max, jnp.max(scores, axis=-1))
        weights = jnp.where(visible_part, jnp.exp(scores - new_max[..., None]), 0.0)
        factor = jnp.exp(running_max - new_max)
        running_sum = running_sum * factor + jnp.sum(weights, axis=-1)
        weighted = weighted * factor[..., None] + jnp.einsum(
            "tgjn,ngd->tgjd",
            weights.astype(jnp.bfloat16),
            value_rows[first_key:last_key],
            preferred_element_type=jnp.float32,
        )
        running_max = new_max
    return (running_max, running_sum, weighted)


def body(
    queries,
    window_keys,
    window_values,
    anchor_keys,
    anchor_values,
    passing_rows,
    block_of_device,
    out_weight,
):
    tok_rows, head_count, head_size = queries.shape
    kv_local = window_keys.shape[1]
    group_size = head_count // kv_local
    retained = passing_rows.shape[1]
    grouped = queries.reshape(tok_rows, kv_local, group_size, head_size)
    my_slot = lax.axis_index("ctx")
    own_block = lookup(block_of_device, jnp.reshape(my_slot, (1,)))[0]
    fold_state = (
        jnp.full((tok_rows, kv_local, group_size), -1e30, jnp.float32),
        jnp.zeros((tok_rows, kv_local, group_size), jnp.float32),
        jnp.zeros((tok_rows, kv_local, group_size, head_size), jnp.float32),
    )
    places = jnp.arange(tok_rows, dtype=jnp.int32)
    causal = places[None, :] <= places[:, None]
    fold_state = attend(fold_state, grouped, window_keys, window_values, causal)
    shard_piece = (
        lax.all_gather(anchor_keys, "ctx", axis=0, tiled=True),
        lax.all_gather(anchor_values, "ctx", axis=0, tiled=True),
    )
    seen_all = jnp.ones((1, shard_piece[0].shape[0]), dtype=bool)
    fold_state = attend(fold_state, grouped, shard_piece[0], shard_piece[1], seen_all)
    chosen = lax.dynamic_slice_in_dim(passing_rows, my_slot, 1, 0)[0]
    picked_keys = jnp.take(window_keys, chosen, axis=0)
    picked_values = jnp.take(window_values, chosen, axis=0)
    shard_piece = (
        lax.all_gather(picked_keys, "ctx", axis=0, tiled=True),
        lax.all_gather(picked_values, "ctx", axis=0, tiled=True),
    )
    rows_here = shard_piece[0].shape[0]
    slot_ids = jnp.arange(rows_here, dtype=jnp.int32) // retained
    earlier = lookup(block_of_device, slot_ids) < own_block
    fold_state = attend(fold_state, grouped, shard_piece[0], shard_piece[1], earlier[None, :])
    running_max, running_sum, weighted = fold_state
    attended = (
        (weighted / running_sum[..., None])
        .reshape(tok_rows, head_count * head_size)
        .astype(jnp.bfloat16)
    )
    return lax.psum_scatter(
        lax.dot_general(
            out_weight, attended, (((1,), (1,)), ((), ())), preferred_element_type=jnp.float32
        ).astype(jnp.bfloat16),
        "tp",
        scatter_dimension=0,
        tiled=True,
    )


def solution(mesh):
    placed = (
        P("ctx", "tp", None),
        P("ctx", "tp", None),
        P("ctx", "tp", None),
        P("ctx", "tp", None),
        P("ctx", "tp", None),
        P(),
        P(),
        P(None, "tp"),
    )
    return jax.shard_map(
        body, mesh=mesh, in_specs=placed, out_specs=P("tp", "ctx"), check_vma=False
    )
```

profile of v0, /device:TPU:0, one launch (start us, length us, event | category | flops | bytes accessed | tf_op | source)
XLA Modules:
  0.0 95.2 jit_solution(17954474765099559327)
XLA Ops:
  6.5 0.0 copy-start
  6.6 0.7 compare_and_fusion
  7.3 1.3 %gather_fusion = bf16[32,128]{1,0:T(8,128)(2,1)S(1)} fusion(bf16[128,128]{1,0:T(8,128)(2,1)} %bitcast.112, s32[1024]{0:T(1024)S(1)} %pad_clamp_fusion), kind=kCustom, calls=%fused_computation.clone | custom fusion | bytes 16512 | tf_op jit(solution)/shard_map/jit(_take)/gather | solution.py:75
  8.7 1.3 %gather_fusion.1 = bf16[32,128]{1,0:T(8,128)(2,1)S(1)} fusion(bf16[128,128]{1,0:T(8,128)(2,1)} %bitcast.114, s32[1024]{0:T(1024)S(1)} %pad_clamp_fusion), kind=kCustom, calls=%fused_computation.1.clone | custom fusion | bytes 16512 | tf_op jit(solution)/shard_map/jit(_take)/gather | solution.py:76
  10.0 0.1 bitcast_select_fusion
  10.1 10.7 %all_gather.14 = bf16[256,1,128]{2,0,1:T(8,128)(2,1)S(1)} all-gather(bf16[32,1,128]{2,0,1:T(8,128)(2,1)S(1)} %get-tuple-element.16), channel_id=1, replica_groups=mesh['ctx'=8,'tp'=4] {'ctx'}, dimensions={0}, use_global_device_ids=true | all-gather | bytes 73728 | tf_op jit(solution)/shard_map/all_gather | solution.py:78
  20.8 1.3 %fusion.44 = s32[]{:T(128)} fusion(s32[8]{0:T(128)} %param.16, s32[]{:T(128)S(6)} %axis_index.15), kind=kLoop, calls=%fused_computation.71 | loop fusion | flops 23 | bytes 40 | tf_op jit(solution)/shard_map/reduce_sum | solution.py:9
  22.1 0.7 select_reduce_fusion
  22.8 9.2 %all_gather.12 = bf16[512,1,128]{2,0,1:T(8,128)(2,1)S(1)} all-gather(bf16[64,1,128]{2,0,1:T(8,128)(2,1)} %param.13), channel_id=1, replica_groups=mesh['ctx'=8,'tp'=4] {'ctx'}, dimensions={0}, use_global_device_ids=true | all-gather | bytes 147456 | tf_op jit(solution)/shard_map/all_gather | solution.py:69
  32.0 0.0 copy-done
  32.0 1.0 %fusion.52 = (f32[128,8]{0,1:T(8,128)S(1)}, f32[128,1,8,128]{0,3,2,1:T(8,128)S(1)}) fusion(bf16[128,8,128]{2,1,0:T(8,128)(2,1)S(1)} %copy-done, bf16[128,1,128]{2,0,1:T(8,128)(2,1)} %param.11, pred[128,128]{0,1:T(8,128)(4,1)S(1)} %iota_compare_fusion), kind=kOutput, calls=%fused_computation.79 | convolution fusion | flops 33946624 | bytes 839680 | tf_op jit(solution)/shard_map/tgjd,ngd->tgjn/dot_general | solution.py:20
  33.0 0.0 slice-start
  33.0 0.4 bitcast_reduce_fusion
  33.5 0.0 copy-start.2
  33.5 8.7 %all_gather.15 = bf16[256,1,128]{2,0,1:T(8,128)(2,1)S(1)} all-gather(bf16[32,1,128]{2,0,1:T(8,128)(2,1)S(1)} %get-tuple-element.15), channel_id=1, replica_groups=mesh['ctx'=8,'tp'=4] {'ctx'}, dimensions={0}, use_global_device_ids=true | all-gather | bytes 73728 | tf_op jit(solution)/shard_map/all_gather | solution.py:79
  42.2 0.6 broadcast_compare_fusion
  42.9 0.3 fusion.51
  43.2 0.2 fusion.20
  43.4 0.3 convolution_bitcast_fusion.1
  43.8 0.0 copy-done.2
  43.8 9.0 %all_gather.13 = bf16[512,1,128]{2,0,1:T(8,128)(2,1)S(1)} all-gather(bf16[64,1,128]{2,0,1:T(8,128)(2,1)S(1)} %copy-done.2), channel_id=1, replica_groups=mesh['ctx'=8,'tp'=4] {'ctx'}, dimensions={0}, use_global_device_ids=true | all-gather | bytes 147456 | tf_op jit(solution)/shard_map/all_gather | solution.py:70
  52.8 0.4 fusion.2
  53.1 0.0 copy-start.1
  53.1 0.5 convolution_bitcast_fusion
  53.7 0.1 fusion.27
  53.8 0.3 copy-done.1
  54.1 0.3 fusion.14
  54.4 0.5 slice-done.1
  55.0 3.8 %fusion = bf16[4096,128]{0,1:T(8,128)(2,1)} fusion(bf16[128,1024]{0,1:T(8,128)(2,1)S(1)} %bitcast.113, bf16[4096,1024]{1,0:T(8,128)(2,1)S(1)} %bitcast.111), kind=kOutput, calls=%fused_computation.3 | convolution fusion | flops 1074266112 | bytes 9699328 | tf_op jit(solution)/shard_map/dot_general | solution.py:92
  58.8 0.0 reduce-scatter.2.cloned.1.call-update
  58.9 27.7 %reduce-scatter.2.cloned.1.call-done = bf16[1024,128]{0,1:T(8,128)(2,1)} async-done(((bf16[4096,128]{0,1:T(8,128)(2,1)}), bf16[1024,128]{0,1:T(8,128)(2,1)}) %reduce-scatter.2.cloned.1.call-update) | async-done | bytes 262160 | tf_op jit(solution)/shard_map/reduce_scatter | solution.py:91
  86.6 1.8 %copy.38 = bf16[1024,128]{1,0:T(8,128)(2,1)} copy(bf16[1024,128]{0,1:T(8,128)(2,1)} %reduce-scatter.2.cloned.1.call-done) | data formatting | bytes 524288 | tf_op jit(solution)/shard_map/reduce_scatter | solution.py:91
  (9 shorter events, 0.1 us)
Async XLA Ops:
  6.5 25.5 %copy-start = (bf16[128,8,128]{2,1,0:T(8,128)(2,1)S(1)}, bf16[128,8,128]{2,1,0:T(8,128)(2,1)}, u32[]{:S(2)}) copy-start(bf16[128,8,128]{2,1,0:T(8,128)(2,1)} %param.10) | copy-start | bytes 786436
  6.5 80.0 %reduce-scatter.2.cloned.1.call-start = ((), (), s32[]{:S(2)}) async-start(), calls=%async_computation.1 | async-start | bytes 1310720 | tf_op jit(solution)/shard_map/reduce_scatter | solution.py:91
  33.0 21.4 %slice-start = ((s8[8388608]{0:T(1024)(128)(4,1)}), s8[4194304]{0:T(1024)(128)(4,1)S(1)}, s32[]{:S(2)}) async-start(s8[8388608]{0:T(1024)(128)(4,1)} %bitcast.110), calls=%async_computation.2 | async-start | bytes 8388608
  33.5 10.3 %copy-start.2 = (bf16[64,1,128]{2,0,1:T(8,128)(2,1)S(1)}, bf16[64,1,128]{2,0,1:T(8,128)(2,1)}, u32[]{:S(2)}) copy-start(bf16[64,1,128]{2,0,1:T(8,128)(2,1)} %param.14) | copy-start | bytes 49156
  52.8 2.2 %slice-start.1 = ((s8[8388608]{0:T(1024)(128)(4,1)}), s8[4194304]{0:T(1024)(128)(4,1)S(1)}, s32[]{:S(2)}) async-start(s8[8388608]{0:T(1024)(128)(4,1)} %bitcast.110), calls=%async_computation.3 | async-start | bytes 8388608
  53.1 0.9 copy-start.1
Sparse Core Ops, SparseCore 0:
  59.0 27.5 reduce-scatter.1
where the time goes:
time: 95.7 us; the launch traced here: 95.2 us
  blocking collectives  37.6 us (39%)
  waiting for transfers between devices  27.7 us (29%)
  between operations  13.5 us (14%)
  matrix products  6.79 us (7%)
  local copies, waits for them, and re-layouts  5.3 us (6%)
  other arithmetic  4.22 us (4%)
    reduce_scatter x1, waiting for transfers between devices, body(): lax.psum_scatter(lax.dot_general(out_weight, attended, (((1,), (1,)), (()...  27.7 us
    all_gather x1, blocking collectives, body(): lax.all_gather(picked_keys, 'ctx', axis=0, tiled=True)  10.7 us
    all_gather x1, blocking collectives, body(): lax.all_gather(anchor_keys, 'ctx', axis=0, tiled=True)  9.17 us
    all_gather x1, blocking collectives, body(): lax.all_gather(anchor_values, 'ctx', axis=0, tiled=True)  9.01 us
    all_gather x1, blocking collectives, body(): lax.all_gather(picked_values, 'ctx', axis=0, tiled=True)  8.72 us
    dot_general x1, matrix products, body(): lax.dot_general(out_weight, attended, (((1,), (1,)), ((), ())), preferred...  3.84 us
    reduce_sum x2, other arithmetic, lookup(): return jnp.sum(jnp.where(matches, lookup_table[None, :], 0), axis=1)  2.03 us
  transfers between devices with their start and end apart: 1, of which 1 were waited for; matrix products, arithmetic and copies ran while one was open for 0% of the time, Pallas kernels for 0%

commit v1 on v0

--- a/solution.py
+++ b/solution.py
@@ -2,6 +2,26 @@
 import jax.numpy as jnp
 from jax import lax
 from jax.sharding import PartitionSpec as P
+
+
+def _prepare_patch(a0):
+    t1, b_now, found_now = (lax.axis_size("ctx"), lax.axis_index("ctx"), a0.shape[0])
+    queue = [jj * t1 if idx == 0 else jj for idx, jj in enumerate(a0.shape)]
+    w2 = lax.dynamic_update_slice_in_dim(jnp.zeros(queue, a0.dtype), a0, b_now * found_now, axis=0)
+    current_value = near = a0
+    for j in [*range(1, t1 // 2 + 1)]:
+        current_value = lax.ppermute(
+            current_value, axis_name="ctx", perm=[(idx, (idx + 1) % t1) for idx in range(t1)]
+        )
+        w2 = lax.dynamic_update_slice_in_dim(
+            w2, current_value, (b_now - j) % t1 * found_now, axis=0
+        )
+        if 2 * j < t1:
+            near = lax.ppermute(
+                near, axis_name="ctx", perm=[(idx, (idx - 1) % t1) for idx in range(t1)]
+            )
+            w2 = lax.dynamic_update_slice_in_dim(w2, near, (b_now + j) % t1 * found_now, axis=0)
+    return w2
 
 
 def lookup(lookup_table, slot_ids):
@@ -67,7 +87,7 @@
     fold_state = attend(fold_state, grouped, window_keys, window_values, causal)
     shard_piece = (
         lax.all_gather(anchor_keys, "ctx", axis=0, tiled=True),
-        lax.all_gather(anchor_values, "ctx", axis=0, tiled=True),
+        _prepare_patch(anchor_values),
     )
     seen_all = jnp.ones((1, shard_piece[0].shape[0]), dtype=bool)
     fold_state = attend(fold_state, grouped, shard_piece[0], shard_piece[1], seen_all)

time: 95.7 us -> 118 us (1.23)
  local copies, waits for them, and re-layouts: 5.3 us -> 23.3 us
  blocking collectives: 37.6 us -> 27.7 us
  starting transfers between devices: 0.01 us -> 7.58 us
  matrix products: 6.79 us -> 10.2 us
  waiting for transfers between devices: 27.7 us -> 30.3 us
    another operation x0 -> x9, local copies, waits for them, and re-layouts: none -> 10.7 us
    all_gather x1 -> x0, blocking collectives: 9.01 us -> none  [body(): lax.all_gather(anchor_values, 'ctx', axis=0, tiled=True)]
    dynamic_update_slice x0 -> x8, local copies, waits for them, and re-layouts: none -> 8.07 us  [the longest x4 3.97 us: _prepare_patch(): lax.dynamic_update_slice_in_dim(w2, current_value, (b_now - j) % t1 * fou...]
    ppermute x0 -> x7, starting transfers between devices: none -> 7.58 us  [the longest x3 6.68 us: _prepare_patch(): lax.ppermute(near, axis_name='ctx', perm=[(idx, (idx - 1) % t1) for idx i...]
    dot_general x1, matrix products: 3.84 us -> 7.27 us  [body(): lax.dot_general(out_weight, attended, (((1,), (1,)), ((), ())), preferred...]
    ppermute x0 -> x7, waiting for transfers between devices: none -> 1.35 us  [the longest x4 1.34 us: _prepare_patch(): lax.ppermute(current_value, axis_name='ctx', perm=[(idx, (idx + 1) % t1)...]
    reduce_scatter x1, waiting for transfers between devices: 27.7 us -> 28.9 us  [body(): lax.psum_scatter(lax.dot_general(out_weight, attended, (((1,), (1,)), (()...]
  transfers between devices with their start and end apart: 1 -> 8, of which waited for: 1 -> 2; matrix products, arithmetic and copies ran while one was open for 0% -> 22% of each run, Pallas kernels for 0% -> 0%
where the time goes in v1:
time: 118 us; the launch traced here: 117 us
  waiting for transfers between devices  30.3 us (26%)
  blocking collectives  27.7 us (23%)
  local copies, waits for them, and re-layouts  23.3 us (20%)
  between operations  13.8 us (12%)
  matrix products  10.2 us (9%)
  starting transfers between devices  7.58 us (6%)
  other arithmetic  4.19 us (4%)
    reduce_scatter x1, waiting for transfers between devices, body(): lax.psum_scatter(lax.dot_general(out_weight, attended, (((1,), (1,)), (()...  28.9 us
    another operation x9, local copies, waits for them, and re-layouts  10.7 us
    all_gather x1, blocking collectives, body(): lax.all_gather(picked_keys, 'ctx', axis=0, tiled=True)  10 us
    all_gather x1, blocking collectives, body(): lax.all_gather(picked_values, 'ctx', axis=0, tiled=True)  9.29 us
    all_gather x1, blocking collectives, body(): lax.all_gather(anchor_keys, 'ctx', axis=0, tiled=True)  8.39 us
    dot_general x1, matrix products, body(): lax.dot_general(out_weight, attended, (((1,), (1,)), ((), ())), preferred...  7.27 us
    ppermute x3, starting transfers between devices, _prepare_patch(): lax.ppermute(near, axis_name='ctx', perm=[(idx, (idx - 1) % t1) for idx i...  6.68 us
    dynamic_update_slice x4, local copies, waits for them, and re-layouts, _prepare_patch(): lax.dynamic_update_slice_in_dim(w2, current_value, (b_now - j) % t1 * fou...  3.97 us
  transfers between devices with their start and end apart: 8, of which 2 were waited for; matrix products, arithmetic and copies ran while one was open for 22% of the time, Pallas kernels for 0%

profile of v1, /device:TPU:0, one launch (start us, length us, event | category | flops | bytes accessed | tf_op | source)
XLA Modules:
  0.0 117.0 jit_solution(3229611965945485571)
XLA Ops:
  7.0 2.9 %collective-permute-start.1 = (bf16[64,1,128]{2,0,1:T(8,128)(2,1)}, bf16[64,1,128]{2,0,1:T(8,128)(2,1)S(1)}, u32[]{:S(2)}, u32[]{:S(2)}) collective-permute-start(bf16[64,1,128]{2,0,1:T(8,128)(2,1)} %param.14), channel_id=1, source_target_pairs={{0,28},{4,0},{8,4},{12,8},{16,12},{20,16},{24,20},{28,24},{1,29},{... | collective-permute-start | bytes 49160 | tf_op jit(solution)/shard_map/ppermute | solution.py:20
  9.9 0.7 compare_and_fusion
  10.6 1.3 %gather_fusion = bf16[32,128]{1,0:T(8,128)(2,1)S(1)} fusion(bf16[128,128]{1,0:T(8,128)(2,1)} %bitcast.114, s32[1024]{0:T(1024)S(1)} %pad_clamp_fusion), kind=kCustom, calls=%fused_computation.clone | custom fusion | bytes 16512 | tf_op jit(solution)/shard_map/jit(_take)/gather | solution.py:95
  12.0 1.3 %gather_fusion.1 = bf16[32,128]{1,0:T(8,128)(2,1)S(1)} fusion(bf16[128,128]{1,0:T(8,128)(2,1)} %bitcast.115, s32[1024]{0:T(1024)S(1)} %pad_clamp_fusion), kind=kCustom, calls=%fused_computation.1.clone | custom fusion | bytes 16512 | tf_op jit(solution)/shard_map/jit(_take)/gather | solution.py:96
  13.4 10.0 %all_gather.10 = bf16[256,1,128]{2,0,1:T(8,128)(2,1)S(1)} all-gather(bf16[32,1,128]{2,0,1:T(8,128)(2,1)S(1)} %get-tuple-element.16), channel_id=1, replica_groups=mesh['ctx'=8,'tp'=4] {'ctx'}, dimensions={0}, use_global_device_ids=true | all-gather | bytes 73728 | tf_op jit(solution)/shard_map/all_gather | solution.py:98
  23.4 1.3 %fusion.44 = s32[]{:T(128)} fusion(s32[8]{0:T(128)} %param.16, s32[]{:T(128)S(6)} %axis_index.19), kind=kLoop, calls=%fused_computation.71 | loop fusion | flops 23 | bytes 40 | tf_op jit(solution)/shard_map/reduce_sum | solution.py:29
  24.7 0.7 select_reduce_fusion
  25.4 8.4 %all_gather.9 = bf16[512,1,128]{2,0,1:T(8,128)(2,1)S(1)} all-gather(bf16[64,1,128]{2,0,1:T(8,128)(2,1)} %param.13), channel_id=1, replica_groups=mesh['ctx'=8,'tp'=4] {'ctx'}, dimensions={0}, use_global_device_ids=true | all-gather | bytes 147456 | tf_op jit(solution)/shard_map/all_gather | solution.py:89
  33.8 1.0 fusion.52
  37.5 2.3 %collective-permute-start.3 = (bf16[64,1,128]{2,0,1:T(8,128)(2,1)S(1)}, bf16[64,1,128]{2,0,1:T(8,128)(2,1)}, u32[]{:S(2)}, u32[]{:S(2)}) collective-permute-start(bf16[64,1,128]{2,0,1:T(8,128)(2,1)S(1)} %collective-permute-done.1), channel_id=1, source_target_pairs={{0,28},{4,0},{8,4},{12,8},{16,12},{20,16},{24,20},{28,24},{1,29},{... | collective-permute-start | bytes 49160 | tf_op jit(solution)/shard_map/ppermute | solution.py:20
  39.8 1.3 %collective-permute-done.2 = bf16[64,1,128]{2,0,1:T(8,128)(2,1)S(1)} collective-permute-done((bf16[64,1,128]{2,0,1:T(8,128)(2,1)S(1)}, bf16[64,1,128]{2,0,1:T(8,128)(2,1)S(1)}, u32[]{:S(2)}, u32[]{:S(2)}) %collective-permute-start.2) | collective-permute-done | bytes 16416 | tf_op jit(solution)/shard_map/ppermute | solution.py:13
  41.4 9.3 %all_gather.11 = bf16[256,1,128]{2,0,1:T(8,128)(2,1)S(1)} all-gather(bf16[32,1,128]{2,0,1:T(8,128)(2,1)S(1)} %get-tuple-element.15), channel_id=1, replica_groups=mesh['ctx'=8,'tp'=4] {'ctx'}, dimensions={0}, use_global_device_ids=true | all-gather | bytes 73728 | tf_op jit(solution)/shard_map/all_gather | solution.py:99
  50.7 1.5 %collective-permute-start.5 = (bf16[64,1,128]{2,0,1:T(8,128)(2,1)}, bf16[64,1,128]{2,0,1:T(8,128)(2,1)}, u32[]{:S(2)}, u32[]{:S(2)}) collective-permute-start(bf16[64,1,128]{2,0,1:T(8,128)(2,1)} %collective-permute-done.3), channel_id=1, source_target_pairs={{0,28},{4,0},{8,4},{12,8},{16,12},{20,16},{24,20},{28,24},{1,29},{... | collective-permute-start | bytes 49160 | tf_op jit(solution)/shard_map/ppermute | solution.py:20
  52.7 0.7 copy.47
  53.4 0.9 dynamic_update_slice.32
  54.4 1.4 %copy.48 = bf16[64,128]{0,1:T(8,128)(2,1)} copy(bf16[64,128]{1,0:T(8,128)(2,1)} %bitcast.118) | data formatting | bytes 32768 | tf_op jit(solution)/shard_map/reshape.150
  55.8 1.4 %copy.49 = bf16[64,128]{0,1:T(8,128)(2,1)} copy(bf16[64,128]{1,0:T(8,128)(2,1)} %bitcast.119) | data formatting | bytes 32768 | tf_op jit(solution)/shard_map/reshape.148
  57.2 1.1 dynamic_update_slice.33
  58.3 1.1 dynamic_update_slice.34
  59.4 1.4 %copy.50 = bf16[64,128]{0,1:T(8,128)(2,1)} copy(bf16[64,128]{1,0:T(8,128)(2,1)} %bitcast.120) | data formatting | bytes 32768 | tf_op jit(solution)/shard_map/reshape.146
  60.9 1.4 %copy.51 = bf16[64,128]{0,1:T(8,128)(2,1)} copy(bf16[64,128]{1,0:T(8,128)(2,1)} %bitcast.17) | data formatting | bytes 32768 | tf_op jit(solution)/shard_map/reshape.144
  62.3 0.9 dynamic_update_slice.35
  63.2 0.9 dynamic_update_slice.36
  64.1 1.4 %copy.52 = bf16[64,128]{0,1:T(8,128)(2,1)} copy(bf16[64,128]{1,0:T(8,128)(2,1)} %bitcast.18) | data formatting | bytes 32768 | tf_op jit(solution)/shard_map/reshape.142
  65.6 1.4 %copy.53 = bf16[64,128]{0,1:T(8,128)(2,1)} copy(bf16[64,128]{1,0:T(8,128)(2,1)} %bitcast.19) | data formatting | bytes 32768 | tf_op jit(solution)/shard_map/reshape.140
  67.0 1.1 dynamic_update_slice.37
  68.1 1.1 dynamic_update_slice.38
  69.2 1.4 %copy.54 = bf16[64,128]{0,1:T(8,128)(2,1)} copy(bf16[64,128]{1,0:T(8,128)(2,1)} %bitcast.20) | data formatting | bytes 32768 | tf_op jit(solution)/shard_map/reshape.115
  70.7 0.9 dynamic_update_slice.39
  72.1 7.3 %fusion = bf16[4096,128]{0,1:T(8,128)(2,1)} fusion(bf16[128,1024]{0,1:T(8,128)(2,1)S(1)} %bitcast.116, bf16[4096,1024]{1,0:T(8,128)(2,1)} %param.17), kind=kOutput, calls=%fused_computation.3 | convolution fusion | flops 1074266112 | bytes 9699328 | tf_op jit(solution)/shard_map/dot_general | solution.py:112
  79.4 28.9 %reduce-scatter.2.cloned.1.call-done = bf16[1024,128]{0,1:T(8,128)(2,1)} async-done(((bf16[4096,128]{0,1:T(8,128)(2,1)}), bf16[1024,128]{0,1:T(8,128)(2,1)}) %reduce-scatter.2.cloned.1.call-update) | async-done | bytes 262160 | tf_op jit(solution)/shard_map/reduce_scatter | solution.py:111
  108.3 1.8 %copy.59 = bf16[1024,128]{1,0:T(8,128)(2,1)} copy(bf16[1024,128]{0,1:T(8,128)(2,1)} %reduce-scatter.2.cloned.1.call-done) | data formatting | bytes 524288 | tf_op jit(solution)/shard_map/reduce_scatter | solution.py:111
  (40 shorter events, 4.3 us)
Async XLA Ops:
  6.5 27.3 %copy-start = (bf16[128,8,128]{2,1,0:T(8,128)(2,1)S(1)}, bf16[128,8,128]{2,1,0:T(8,128)(2,1)}, u32[]{:S(2)}) copy-start(bf16[128,8,128]{2,1,0:T(8,128)(2,1)} %param.10) | copy-start | bytes 786436
  6.5 101.8 %reduce-scatter.2.cloned.1.call-start = ((), (), s32[]{:S(2)}) async-start(), calls=%async_computation.1 | async-start | bytes 1310720 | tf_op jit(solution)/shard_map/reduce_scatter | solution.py:111
  6.5 30.5 %collective-permute-start = (bf16[64,1,128]{2,0,1:T(8,128)(2,1)}, bf16[64,1,128]{2,0,1:T(8,128)(2,1)S(1)}, u32[]{:S(2)}, u32[]{:S(2)}) collective-permute-start(bf16[64,1,128]{2,0,1:T(8,128)(2,1)} %param.14), channel_id=1, source_target_pairs={{0,4},{4,8},{8,12},{12,16},{16,20},{20,24},{24,28},{28,0},{1,5},{5... | collective-permute-start | bytes 49160 | tf_op jit(solution)/shard_map/ppermute | solution.py:13
  7.0 30.4 %collective-permute-start.1 = (bf16[64,1,128]{2,0,1:T(8,128)(2,1)}, bf16[64,1,128]{2,0,1:T(8,128)(2,1)S(1)}, u32[]{:S(2)}, u32[]{:S(2)}) collective-permute-start(bf16[64,1,128]{2,0,1:T(8,128)(2,1)} %param.14), channel_id=1, source_target_pairs={{0,28},{4,0},{8,4},{12,8},{16,12},{20,16},{24,20},{28,24},{1,29},{... | collective-permute-start | bytes 49160 | tf_op jit(solution)/shard_map/ppermute | solution.py:20
  36.3 4.9 %copy-start.1 = (bf16[128,1,128]{2,0,1:T(8,128)(2,1)S(1)}, bf16[128,1,128]{2,0,1:T(8,128)(2,1)}, u32[]{:S(2)}) copy-start(bf16[128,1,128]{2,0,1:T(8,128)(2,1)} %param.12) | copy-start | bytes 98308
  36.9 15.8 %copy-start.2 = (bf16[64,1,128]{2,0,1:T(8,128)(2,1)S(1)}, bf16[64,1,128]{2,0,1:T(8,128)(2,1)}, u32[]{:S(2)}) copy-start(bf16[64,1,128]{2,0,1:T(8,128)(2,1)} %param.14) | copy-start | bytes 49156
  37.0 16.4 %copy-start.3 = (bf16[64,1,128]{2,0,1:T(8,128)(2,1)}, bf16[64,1,128]{2,0,1:T(8,128)(2,1)S(1)}, u32[]{:S(2)}) copy-start(bf16[64,1,128]{2,0,1:T(8,128)(2,1)S(1)} %collective-permute-done) | copy-start | bytes 49156
  37.0 4.1 %collective-permute-start.2 = (bf16[64,1,128]{2,0,1:T(8,128)(2,1)S(1)}, bf16[64,1,128]{2,0,1:T(8,128)(2,1)S(1)}, u32[]{:S(2)}, u32[]{:S(2)}) collective-permute-start(bf16[64,1,128]{2,0,1:T(8,128)(2,1)S(1)} %collective-permute-done), channel_id=1, source_target_pairs={{0,4},{4,8},{8,12},{12,16},{16,20},{20,24},{24,28},{28,0},{1,5},{5... | collective-permute-start | bytes 49160 | tf_op jit(solution)/shard_map/ppermute | solution.py:13
  37.5 16.0 %copy-start.4 = (bf16[64,1,128]{2,0,1:T(8,128)(2,1)}, bf16[64,1,128]{2,0,1:T(8,128)(2,1)S(1)}, u32[]{:S(2)}) copy-start(bf16[64,1,128]{2,0,1:T(8,128)(2,1)S(1)} %collective-permute-done.1) | copy-start | bytes 49156
  37.5 13.3 %collective-permute-start.3 = (bf16[64,1,128]{2,0,1:T(8,128)(2,1)S(1)}, bf16[64,1,128]{2,0,1:T(8,128)(2,1)}, u32[]{:S(2)}, u32[]{:S(2)}) collective-permute-start(bf16[64,1,128]{2,0,1:T(8,128)(2,1)S(1)} %collective-permute-done.1), channel_id=1, source_target_pairs={{0,28},{4,0},{8,4},{12,8},{16,12},{20,16},{24,20},{28,24},{1,29},{... | collective-permute-start | bytes 49160 | tf_op jit(solution)/shard_map/ppermute | solution.py:20
  41.1 12.3 %copy-start.5 = (bf16[64,1,128]{2,0,1:T(8,128)(2,1)}, bf16[64,1,128]{2,0,1:T(8,128)(2,1)S(1)}, u32[]{:S(2)}) copy-start(bf16[64,1,128]{2,0,1:T(8,128)(2,1)S(1)} %collective-permute-done.2) | copy-start | bytes 49156
  41.1 11.0 %collective-permute-start.4 = (bf16[64,1,128]{2,0,1:T(8,128)(2,1)S(1)}, bf16[64,1,128]{2,0,1:T(8,128)(2,1)}, u32[]{:S(2)}, u32[]{:S(2)}) collective-permute-start(bf16[64,1,128]{2,0,1:T(8,128)(2,1)S(1)} %collective-permute-done.2), channel_id=1, source_target_pairs={{0,4},{4,8},{8,12},{12,16},{16,20},{20,24},{24,28},{28,0},{1,5},{5... | collective-permute-start | bytes 49160 | tf_op jit(solution)/shard_map/ppermute | solution.py:13
  50.7 14.8 %collective-permute-start.5 = (bf16[64,1,128]{2,0,1:T(8,128)(2,1)}, bf16[64,1,128]{2,0,1:T(8,128)(2,1)}, u32[]{:S(2)}, u32[]{:S(2)}) collective-permute-start(bf16[64,1,128]{2,0,1:T(8,128)(2,1)} %collective-permute-done.3), channel_id=1, source_target_pairs={{0,28},{4,0},{8,4},{12,8},{16,12},{20,16},{24,20},{28,24},{1,29},{... | collective-permute-start | bytes 49160 | tf_op jit(solution)/shard_map/ppermute | solution.py:20
  52.2 17.0 %collective-permute-start.6 = (bf16[64,1,128]{2,0,1:T(8,128)(2,1)}, bf16[64,1,128]{2,0,1:T(8,128)(2,1)}, u32[]{:S(2)}, u32[]{:S(2)}) collective-permute-start(bf16[64,1,128]{2,0,1:T(8,128)(2,1)} %collective-permute-done.4), channel_id=1, source_target_pairs={{0,4},{4,8},{8,12},{12,16},{16,20},{20,24},{24,28},{28,0},{1,5},{5... | collective-permute-start | bytes 49160 | tf_op jit(solution)/shard_map/ppermute | solution.py:13
Sparse Core Ops, SparseCore 0:
  79.5 28.7 reduce-scatter.1
